TPU v7x, 32 devices: a whole 2x2x4 slice. The times are simulated.
32 devices in a mesh: ord: 4 (over x, core), blk: 8 (over z, y).
Axes of the slice: x: 2, y: 2, z: 4, core: 2. Of those that a mesh axis runs over, the one named last changes fastest.
Arguments:
- coefficients: bfloat16 [32, 2, 256, 4096], P('ord', None, None, 'blk'), may hold values from -1.0546875 to 1.0546875
- leaf_factors: bfloat16 [32, 128, 4096], P('ord', None, 'blk'), may hold values from -0.25 to 0.25
- level_interpolants: bfloat16 [3, 2, 32, 128, 1024], P(None, None, 'ord', None, 'blk'), may hold values from -0.375 to 0.375
- latitude_factors: bfloat16 [32, 5120, 128], P('ord', 'blk'), may hold values from -0.5 to 0.5
- order_ids: int32 [32], replicated, may hold values from 0 to 8191, as said below
Outputs:
- products: bfloat16 [256, 128, 5120], P(None, 'ord', 'blk')
Inputs may be any that keep to these rules, and one draw needn't show every extreme that they name: `order_ids`: the slots hold distinct orders of the truncation.
All inputs are finite; a program needn't handle non-finite values.
Results may differ from a plain program's by a relative error of at most 0.011.
Values may be sent and summed in bfloat16 or wider, within the bound.
A program may use at most 128 MiB of HBM per device.

v0:
```python
import math

import jax
import jax.numpy as jnp
from jax import lax
from jax.sharding import PartitionSpec as P

PERIOD = 16384
NLON = 256


def partner(shard, axis, apart):
    return lax.ppermute(shard, axis, [(i, i ^ 1 << apart) for i in range(lax.axis_size(axis))])


def synthesis_table(order_ids, count, period):
    steps = jnp.arange(count, dtype=jnp.int32)
    phase = (order_ids[:, None] * steps[None, :] % period).astype(jnp.float32) * (
        2.0 * math.pi / period
    )
    weight = jnp.where(order_ids == 0, 1.0, 2.0).astype(jnp.float32)[:, None]
    table = jnp.stack([weight * jnp.cos(phase), -weight * jnp.sin(phase)], axis=1)
    return table.astype(jnp.bfloat16)


def per_device(coefficients, leaf_factors, level_interpolants, latitude_factors, order_ids):
    orders_here, parts, fields, leaf = coefficients.shape
    flat = coefficients.reshape(orders_here, parts * fields, leaf)
    combined_sum = jnp.einsum(
        "mcl,mrl->mcr", flat, leaf_factors, preferred_element_type=jnp.float32
    ).astype(jnp.bfloat16)
    level_count = level_interpolants.shape[0]
    top_bit = lax.axis_size("blk").bit_length() - 1
    for tree_level in range(level_count):
        partner_block = partner(combined_sum, "blk", top_bit - 1 - tree_level)
        mixed = jnp.einsum(
            "dfx,dhx->dfh",
            combined_sum,
            level_interpolants[tree_level, 0],
            preferred_element_type=jnp.float32,
        )
        mixed = mixed + jnp.einsum(
            "dfx,dhx->dfh",
            partner_block,
            level_interpolants[tree_level, 1],
            preferred_element_type=jnp.float32,
        )
        combined_sum = mixed.astype(jnp.bfloat16)
    rank = combined_sum.shape[2]
    spaced = combined_sum.reshape(orders_here, parts, fields, rank)
    collected_rows = lax.all_to_all(spaced, "ord", split_axis=2, concat_axis=0, tiled=True)
    mapped = jnp.einsum(
        "mrfk,mlk->mrfl",
        collected_rows,
        lax.all_gather(latitude_factors, "ord", axis=0, tiled=True),
        preferred_element_type=jnp.float32,
    )
    regrouped = mapped.astype(jnp.bfloat16)
    total_orders, parts_again, group, lat_count = regrouped.shape
    table = synthesis_table(order_ids, NLON, PERIOD).reshape(total_orders * parts_again, NLON)
    stacked_blocks = regrouped.reshape(total_orders * parts_again, group * lat_count)
    grid = lax.dot_general(
        table, stacked_blocks, (((0,), (0,)), ((), ())), preferred_element_type=jnp.float32
    )
    grid = grid.reshape(NLON, group // 2, 2, lat_count)
    return (grid[:, :, 0, :] * grid[:, :, 1, :]).astype(jnp.bfloat16)


def solution(mesh):
    in_specs = (
        P("ord", None, None, "blk"),
        P("ord", None, "blk"),
        P(None, None, "ord", None, "blk"),
        P("ord", "blk", None),
        P(),
    )
    out_specs = P(None, "ord", "blk")
    return jax.shard_map(
        per_device, mesh=mesh, in_specs=in_specs, out_specs=out_specs, check_vma=False
    )
```

profile of v0, /device:TPU:0, one launch (start us, length us, event | category | flops | bytes accessed | tf_op | source)
XLA Modules:
  0.0 213.8 jit_solution(15149191773812317247)
XLA Ops:
  6.5 0.7 all-gather.2.cloned.1.call-update
  7.3 0.5 copy-done
  7.8 3.6 %convolution_convert_fusion = bf16[8,512,128]{2,1,0:T(8,128)(2,1)S(1)} fusion(bf16[8,512,512]{2,1,0:T(8,128)(2,1)} %bitcast.57, bf16[8,128,512]{2,1,0:T(8,128)(2,1)S(1)} %copy-done), kind=kOutput, calls=%fused_computation.11 | convolution fusion | flops 537395200 | bytes 6291456 | tf_op jit(solution)/shard_map/mcl,mrl->mcr/dot_general | solution.py:29
  11.3 4.1 %collective-permute-start = (bf16[8,512,128]{2,1,0:T(8,128)(2,1)S(1)}, bf16[8,512,128]{2,1,0:T(8,128)(2,1)S(1)}, u32[]{:S(2)}, u32[]{:S(2)}) collective-permute-start(bf16[8,512,128]{2,1,0:T(8,128)(2,1)S(1)} %convolution_convert_fusion), channel_id=1, source_target_pairs={{0,4},{1,5},{2,6},{3,7},{4,0},{5,1},{6,2},{7,3},{8,12},{9,13},{10,... | collective-permute-start | bytes 3145736 | tf_op jit(solution)/shard_map/ppermute | solution.py:13
  15.5 0.4 fusion.16
  15.9 45.2 %collective-permute-done = bf16[8,512,128]{2,1,0:T(8,128)(2,1)S(1)} collective-permute-done((bf16[8,512,128]{2,1,0:T(8,128)(2,1)S(1)}, bf16[8,512,128]{2,1,0:T(8,128)(2,1)S(1)}, u32[]{:S(2)}, u32[]{:S(2)}) %collective-permute-start) | collective-permute-done | bytes 1048608 | tf_op jit(solution)/shard_map/ppermute | solution.py:13
  61.1 0.4 add_convert_fusion.2
  61.5 0.8 collective-permute-start.1
  62.3 0.4 fusion.13
  62.8 23.2 %collective-permute-done.1 = bf16[8,512,128]{2,1,0:T(8,128)(2,1)S(1)} collective-permute-done((bf16[8,512,128]{2,1,0:T(8,128)(2,1)S(1)}, bf16[8,512,128]{2,1,0:T(8,128)(2,1)S(1)}, u32[]{:S(2)}, u32[]{:S(2)}) %collective-permute-start.1) | collective-permute-done | bytes 1048608 | tf_op jit(solution)/shard_map/ppermute | solution.py:13
  85.9 0.4 add_convert_fusion.1
  86.4 1.4 collective-permute-start.2
  87.7 0.4 fusion.10
  88.2 21.7 %collective-permute-done.2 = bf16[8,512,128]{2,1,0:T(8,128)(2,1)S(1)} collective-permute-done((bf16[8,512,128]{2,1,0:T(8,128)(2,1)S(1)}, bf16[8,512,128]{2,1,0:T(8,128)(2,1)S(1)}, u32[]{:S(2)}, u32[]{:S(2)}) %collective-permute-start.2) | collective-permute-done | bytes 1048608 | tf_op jit(solution)/shard_map/ppermute | solution.py:13
  109.9 0.4 add_convert_fusion
  110.4 2.0 copy.20
  112.4 3.5 %all-to-all-start = ((bf16[8,2,256,128]{3,1,0,2:T(2,128)(2,1)}), bf16[8,2,256,128]{3,1,0,2:T(2,128)(2,1)S(1)}, u32[]{:S(2)}, u32[]{:S(2)}) async-start(bf16[8,2,256,128]{3,1,0,2:T(2,128)(2,1)} %copy.20), calls=%async_computation | async-start | bytes 2097152 | tf_op jit(solution)/shard_map/all_to_all | solution.py:51
  116.2 14.1 %all-to-all-done = bf16[8,2,256,128]{3,1,0,2:T(2,128)(2,1)S(1)} async-done(((bf16[8,2,256,128]{3,1,0,2:T(2,128)(2,1)}), bf16[8,2,256,128]{3,1,0,2:T(2,128)(2,1)S(1)}, u32[]{:S(2)}, u32[]{:S(2)}) %all-to-all-start) | async-done | bytes 1048608 | tf_op jit(solution)/shard_map/all_to_all | solution.py:51
  130.6 4.5 %fusion.6 = bf16[32,2,64,640]{3,2,1,0:T(8,128)(2,1)S(1)} fusion(bf16[32,2,64,128]{3,2,1,0:T(8,128)(2,1)S(1)} %bitcast.56, bf16[32,640,128]{2,1,0:T(8,128)(2,1)} %all-gather.2.cloned.1.call-done), kind=kOutput, calls=%fused_computation.7 | convolution fusion | flops 673710080 | bytes 11534336 | tf_op jit(solution)/shard_map/mrfk,mlk->mrfl/dot_general | solution.py:52
  135.1 5.6 %copy.26 = bf16[8,8,64,640]{3,1,2,0:T(8,128)(2,1)} copy(bf16[8,8,64,640]{3,2,1,0:T(8,128)(2,1)S(1)} %bitcast.52) | data formatting | bytes 10485760
  140.7 8.7 %dot_general.40 = bf16[32,2,640,64]{2,1,0,3:T(2,128)(2,1)} reshape(bf16[40960,64]{0,1:T(8,128)(2,1)} %bitcast.53) | data formatting | bytes 10485760 | tf_op jit(solution)/shard_map/dot_general | solution.py:62
  149.4 24.9 %fusion.4 = f32[256,32,2,640]{3,0,2,1:T(8,128)} fusion(bf16[32,2,640,64]{2,1,0,3:T(2,128)(2,1)} %dot_general.40, bf16[64,256,1,1]{1,0,2,3:T(8,128)(2,1)S(1)} %reshape.160), kind=kOutput, calls=%fused_computation.5 | convolution fusion | flops 1342177280 | bytes 47218688 | tf_op jit(solution)/shard_map/dot_general | solution.py:62
  174.3 18.4 %fusion.1 = bf16[256,32,640]{2,0,1:T(8,128)(2,1)} fusion(f32[256,32,2,640]{3,0,2,1:T(8,128)} %fusion.4), kind=kLoop, calls=%fused_computation.2 | loop fusion | flops 10485760 | bytes 52428800 | tf_op jit(solution)/shard_map/convert_element_type | solution.py:66
  192.7 14.2 %copy.23 = bf16[256,32,640]{2,1,0:T(8,128)(2,1)} copy(bf16[256,32,640]{2,0,1:T(8,128)(2,1)} %fusion.1) | data formatting | bytes 20971520 | tf_op jit(solution)/shard_map/convert_element_type | solution.py:66
  (15 shorter events, 0.6 us)
Async XLA Ops:
  6.5 1.2 copy-start
  6.5 124.1 %all-gather.2.cloned.1.call-start = ((), (), s32[]{:S(2)}) async-start(), calls=%async_computation.1 | async-start | bytes 6553600 | tf_op jit(solution)/shard_map/all_gather | solution.py:55
  7.8 7.7 %copy-start.2 = (bf16[3,2,8,128,128]{4,3,2,1,0:T(8,128)(2,1)S(1)}, bf16[3,2,8,128,128]{4,3,2,1,0:T(8,128)(2,1)}, u32[]{:S(2)}) copy-start(bf16[3,2,8,128,128]{4,3,2,1,0:T(8,128)(2,1)} %param.7) | copy-start | bytes 4718596
  11.3 49.8 %collective-permute-start = (bf16[8,512,128]{2,1,0:T(8,128)(2,1)S(1)}, bf16[8,512,128]{2,1,0:T(8,128)(2,1)S(1)}, u32[]{:S(2)}, u32[]{:S(2)}) collective-permute-start(bf16[8,512,128]{2,1,0:T(8,128)(2,1)S(1)} %convolution_convert_fusion), channel_id=1, source_target_pairs={{0,4},{1,5},{2,6},{3,7},{4,0},{5,1},{6,2},{7,3},{8,12},{9,13},{10,... | collective-permute-start | bytes 3145736 | tf_op jit(solution)/shard_map/ppermute | solution.py:13
  61.5 24.4 %collective-permute-start.1 = (bf16[8,512,128]{2,1,0:T(8,128)(2,1)S(1)}, bf16[8,512,128]{2,1,0:T(8,128)(2,1)S(1)}, u32[]{:S(2)}, u32[]{:S(2)}) collective-permute-start(bf16[8,512,128]{2,1,0:T(8,128)(2,1)S(1)} %add_convert_fusion.2), channel_id=1, source_target_pairs={{0,2},{1,3},{2,0},{3,1},{4,6},{5,7},{6,4},{7,5},{8,10},{9,11},{10,... | collective-permute-start | bytes 3145736 | tf_op jit(solution)/shard_map/ppermute | solution.py:13
  86.4 23.5 %collective-permute-start.2 = (bf16[8,512,128]{2,1,0:T(8,128)(2,1)S(1)}, bf16[8,512,128]{2,1,0:T(8,128)(2,1)S(1)}, u32[]{:S(2)}, u32[]{:S(2)}) collective-permute-start(bf16[8,512,128]{2,1,0:T(8,128)(2,1)S(1)} %add_convert_fusion.1), channel_id=1, source_target_pairs={{0,1},{1,0},{2,3},{3,2},{4,5},{5,4},{6,7},{7,6},{8,9},{9,8},{10,11... | collective-permute-start | bytes 3145736 | tf_op jit(solution)/shard_map/ppermute | solution.py:13
  110.3 5.6 %copy-start.3 = (s32[32]{0:T(128)S(1)}, s32[32]{0:T(128)}, u32[]{:S(2)}) copy-start(s32[32]{0:T(128)} %param.9) | copy-start | bytes 388
  112.4 17.9 %all-to-all-start = ((bf16[8,2,256,128]{3,1,0,2:T(2,128)(2,1)}), bf16[8,2,256,128]{3,1,0,2:T(2,128)(2,1)S(1)}, u32[]{:S(2)}, u32[]{:S(2)}) async-start(bf16[8,2,256,128]{3,1,0,2:T(2,128)(2,1)} %copy.20), calls=%async_computation | async-start | bytes 2097152 | tf_op jit(solution)/shard_map/all_to_all | solution.py:51
  192.7 14.2 %copy-start.1 = (bf16[8,128,512]{2,1,0:T(8,128)(2,1)S(1)}, bf16[8,128,512]{2,1,0:T(8,128)(2,1)}, u32[]{:S(2)}) copy-start(bf16[8,128,512]{2,1,0:T(8,128)(2,1)} %param.6) | copy-start | bytes 3145732
Sparse Core Ops, SparseCore 0:
  8.9 43.1 all-gather.1
where the time goes:
time: 214 us
  waiting for transfers between devices  105 us (49%)
  matrix products  35.5 us (17%)
  local copies, waits for them, and re-layouts  31.4 us (15%)
  other arithmetic  18.6 us (9%)
  between operations  13.5 us (6%)
  starting transfers between devices  9.81 us (5%)
    ppermute x3, waiting for transfers between devices, partner(): lax.ppermute(shard, axis, [(i, i ^ 1 << apart) for i in range(lax.axis_si...  90.1 us
    dot_general x1, matrix products, per_device(): lax.dot_general(table, stacked_blocks, (((0,), (0,)), ((), ())), preferre...  24.9 us
    convert_element_type x1, other arithmetic, per_device(): return (grid[:, :, 0, :] * grid[:, :, 1, :]).astype(jnp.bfloat16)  18.4 us
    convert_element_type x1, local copies, waits for them, and re-layouts, per_device(): return (grid[:, :, 0, :] * grid[:, :, 1, :]).astype(jnp.bfloat16)  14.2 us
    all_to_all x1, waiting for transfers between devices, per_device(): lax.all_to_all(spaced, 'ord', split_axis=2, concat_axis=0, tiled=True)  14.1 us
    dot_general x1, local copies, waits for them, and re-layouts, per_device(): lax.dot_general(table, stacked_blocks, (((0,), (0,)), ((), ())), preferre...  8.72 us
    ppermute x3, starting transfers between devices, partner(): lax.ppermute(shard, axis, [(i, i ^ 1 << apart) for i in range(lax.axis_si...  6.29 us
    unnamed x9, local copies, waits for them, and re-layouts  6.1 us
  transfers between devices with their start and end apart: 5, of which 4 were waited for; matrix products, arithmetic and copies ran while one was open for 4% of the time, Pallas kernels for 0%

commit v1 on v0

v1 whole, which is shorter than its diff:
```python
import functools
import math

import jax
import jax.numpy as jnp
from jax import lax
from jax.experimental import pallas as pl
from jax.experimental.pallas import tpu as pltpu
from jax.sharding import PartitionSpec as P

PERIOD = 16384
NLON = 256
LANES = 128
WINDOW = 2
LEVEL_LAG = 1
MESH = pl.DeviceIdType.MESH
NT = (((1,), (1,)), ((), ()))


def synthesis_table(order_ids, count, period):
    steps = jnp.arange(count, dtype=jnp.int32)
    phase = (steps[:, None] * order_ids[None, :] % period).astype(jnp.float32) * (
        2.0 * math.pi / period
    )
    weight = jnp.where(order_ids == 0, 1.0, 2.0).astype(jnp.float32)[None, :]
    table = jnp.stack([weight * jnp.cos(phase), -weight * jnp.sin(phase)], axis=2)
    return table.astype(jnp.bfloat16).reshape(count, -1)


def butterfly_kernel(
    n_ord, n_blk, coef_hbm, leaf_hbm, interp_hbm, lat_hbm,
    rows_out, lat_out,
    coef, leaf, interp, lat, own, came,
    in_sem, level_send, level_recv, group_send, group_recv, own_sem,
    lat_send, lat_recv, lat_pass,
):
    me_ord, me_blk = lax.axis_index("ord"), lax.axis_index("blk")
    orders, columns, _ = coef.shape
    levels = interp.shape[0]
    parts, _, group, rank = rows_out.shape[1], None, rows_out.shape[2], rows_out.shape[3]

    lat_in = pltpu.make_async_copy(lat_hbm, lat, in_sem.at[2, 0])
    interp_in = pltpu.make_async_copy(interp_hbm, interp, in_sem.at[2, 1])

    def order_in(i):
        return (
            pltpu.make_async_copy(coef_hbm.at[i], coef.at[i], in_sem.at[0, i]),
            pltpu.make_async_copy(leaf_hbm.at[i], leaf.at[i], in_sem.at[1, i]),
        )

    for i in range(orders):
        for copy in order_in(i):
            copy.start()
        if i == 1:
            lat_in.start()
            interp_in.start()

    barrier = pltpu.get_barrier_semaphore()
    partners = [me_blk ^ (n_blk >> (k + 1)) for k in range(levels)]
    for k in range(levels):
        pl.semaphore_signal(barrier, inc=1, device_id={"blk": partners[k]}, device_id_type=MESH)
    peers = [lax.rem(me_ord + d, n_ord) for d in range(1, n_ord)]
    for peer in peers:
        pl.semaphore_signal(barrier, inc=1, device_id={"ord": peer}, device_id_type=MESH)
    pl.semaphore_wait(barrier, levels + n_ord - 1)

    def level_copy(k, i):
        return pltpu.make_async_remote_copy(
            src_ref=own.at[k, i], dst_ref=came.at[k, i],
            send_sem=level_send.at[k, i], recv_sem=level_recv.at[k, i],
            device_id={"blk": partners[k]}, device_id_type=MESH,
        )

    def group_copy(i, d):
        peer = lax.rem(me_ord + d, n_ord)
        return pltpu.make_async_remote_copy(
            src_ref=own_groups(i, peer), dst_ref=rows_out.at[me_ord * orders + i],
            send_sem=group_send.at[i, d], recv_sem=group_recv.at[i, d],
            device_id={"ord": peer}, device_id_type=MESH,
        )

    def own_groups(i, g):
        return own.at[levels, i].reshape(parts, n_ord, group, rank).at[:, g]

    def own_copy(i):
        return pltpu.make_async_copy(
            own_groups(i, me_ord), rows_out.at[me_ord * orders + i], own_sem.at[i]
        )

    def lat_rows(o):
        return lat_out.at[pl.ds(o * orders, orders)]

    half = n_ord // 2
    mate = me_ord ^ 1

    def lat_copy(d):
        target = mate if d == 0 else lax.rem(me_ord + 2 * d, n_ord)
        return pltpu.make_async_remote_copy(
            src_ref=lat, dst_ref=lat_rows(me_ord),
            send_sem=lat_send.at[d], recv_sem=lat_recv.at[d],
            device_id={"ord": target}, device_id_type=MESH,
        )

    def lat_forward(d):
        source = lax.rem(me_ord + n_ord - 2 * d, n_ord)
        return pltpu.make_async_remote_copy(
            src_ref=lat_rows(source), dst_ref=lat_rows(source),
            send_sem=lat_pass.at[d], recv_sem=lat_recv.at[half + d],
            device_id={"ord": mate}, device_id_type=MESH,
        )

    lat_own = pltpu.make_async_copy(lat, lat_rows(me_ord), in_sem.at[2, 2])

    def leaf_step(i):
        for copy in order_in(i):
            copy.wait()
        own[0, i] = lax.dot_general(
            coef[i], leaf[i], NT, preferred_element_type=jnp.float32
        ).astype(jnp.bfloat16)

    for i in range(WINDOW):
        leaf_step(i)
        level_copy(0, i).start()
    lat_in.wait()
    for d in range(half):
        lat_copy(d).start()
    lat_own.start()

    @pl.loop(WINDOW, orders)
    def _(i):
        leaf_step(i)

    interp_in.wait()

    def level_step(k, i):
        level_copy(k, i).wait_recv()
        mixed = lax.dot_general(
            own[k, i], interp[k, 0, i], NT, preferred_element_type=jnp.float32
        ) + lax.dot_general(
            came[k, i], interp[k, 1, i], NT, preferred_element_type=jnp.float32
        )
        own[k + 1, i] = mixed.astype(jnp.bfloat16)
        if k + 1 < levels:
            level_copy(k + 1, i).start()
        else:
            for d in range(1, n_ord):
                group_copy(i, d).start()
            own_copy(i).start()

    steps = orders + LEVEL_LAG * (levels - 1)

    @pl.loop(0, steps)
    def _(s):
        for k in range(levels):
            i = s - k * LEVEL_LAG

            @pl.when((i >= 0) & (i < orders))
            def _():
                level_step(k, i)
                if k == 0:
                    @pl.when(i + WINDOW < orders)
                    def _():
                        level_copy(0, i + WINDOW).start()

        @pl.when(s == orders - 1)
        def _():
            for d in range(1, half):
                lat_copy(d).wait_recv()
                lat_forward(d).start()

    lat_copy(0).wait_recv()
    for d in range(1, half):
        lat_forward(d).wait_recv()
    for d in range(half):
        lat_copy(d).wait_send()
    for d in range(1, half):
        lat_forward(d).wait_send()
    lat_own.wait()

    @pl.loop(0, orders)
    def _(i):
        for k in range(levels):
            level_copy(k, i).wait_send()
        for d in range(1, n_ord):
            group_copy(i, d).wait_recv()
            group_copy(i, d).wait_send()
        own_copy(i).wait()


def butterfly(flat, leaf_factors, interpolants, latitude_factors, parts, n_ord, n_blk):
    orders, columns, _ = flat.shape
    rank = leaf_factors.shape[1]
    levels = interpolants.shape[0]
    lats = latitude_factors.shape[1]
    group = columns // parts // n_ord
    any_spec = pl.BlockSpec(memory_space=pl.ANY)
    dma = pltpu.SemaphoreType.DMA
    return pl.pallas_call(
        functools.partial(butterfly_kernel, n_ord, n_blk),
        out_shape=(
            jax.ShapeDtypeStruct((n_ord * orders, parts, group, rank), jnp.bfloat16),
            jax.ShapeDtypeStruct((n_ord * orders, lats, rank), jnp.bfloat16),
        ),
        in_specs=[any_spec] * 4,
        out_specs=(any_spec, any_spec),
        scratch_shapes=[
            pltpu.VMEM(flat.shape, jnp.bfloat16),
            pltpu.VMEM(leaf_factors.shape, jnp.bfloat16),
            pltpu.VMEM(interpolants.shape, jnp.bfloat16),
            pltpu.VMEM(latitude_factors.shape, jnp.bfloat16),
            pltpu.VMEM((levels + 1, orders, columns, rank), jnp.bfloat16),
            pltpu.VMEM((levels, orders, columns, rank), jnp.bfloat16),
            dma((3, max(orders, 3))),
            dma((levels, orders)),
            dma((levels, orders)),
            dma((orders, n_ord)),
            dma((orders, n_ord)),
            dma((orders,)),
            dma((n_ord,)),
            dma((n_ord,)),
            dma((n_ord,)),
        ],
        compiler_params=pltpu.CompilerParams(collective_id=0, has_side_effects=True),
        name="butterfly",
    )(flat, leaf_factors, interpolants, latitude_factors)


def products_kernel(table_ref, rows_ref, lat_ref, out_ref, values, mixed):
    total, parts, group, rank = rows_ref.shape
    nlon, pairs, lanes = out_ref.shape
    depth = total * parts

    @pl.loop(0, total, unroll=4)
    def _(m):
        at = pl.multiple_of(m * parts * group, parts * group)
        values[pl.ds(at, parts * group), :] = lax.dot_general(
            rows_ref[m].reshape(parts * group, rank), lat_ref[m], NT,
            preferred_element_type=jnp.float32,
        )

    @pl.loop(0, pairs, unroll=2)
    def _(p):
        both = jnp.concatenate(
            [values[pl.ds(2 * p + h, depth, stride=group), :].astype(jnp.bfloat16) for h in range(2)],
            axis=1,
        )
        grid = jnp.dot(table_ref[...], both, preferred_element_type=jnp.float32)
        mixed[pl.ds(p, nlon, stride=pairs), :] = grid[:, :lanes] * grid[:, lanes:]

    @pl.loop(0, nlon // 16, unroll=2)
    def _(b):
        at = pl.multiple_of(b * 16 * pairs, 16 * pairs)
        out_ref[pl.ds(b * 16, 16)] = (
            mixed[pl.ds(at, 16 * pairs), :].astype(jnp.bfloat16).reshape(16, pairs, lanes)
        )


def products_of(table, rows, lat):
    total, parts, group, rank = rows.shape
    lats = lat.shape[1]
    pairs = group // 2
    nlon = table.shape[0]
    return pl.pallas_call(
        products_kernel,
        out_shape=jax.ShapeDtypeStruct((nlon, pairs, lats), jnp.bfloat16),
        grid=(lats // LANES,),
        in_specs=[
            pl.BlockSpec(table.shape, lambda t: (0, 0)),
            pl.BlockSpec(rows.shape, lambda t: (0, 0, 0, 0)),
            pl.BlockSpec((total, LANES, rank), lambda t: (0, t, 0)),
        ],
        out_specs=pl.BlockSpec((nlon, pairs, LANES), lambda t: (0, 0, t)),
        scratch_shapes=[
            pltpu.VMEM((total * parts * group, LANES), jnp.float32),
            pltpu.VMEM((nlon * pairs, LANES), jnp.float32),
        ],
        name="products",
    )(table, rows, lat)


def per_device(coefficients, leaf_factors, level_interpolants, latitude_factors, order_ids):
    orders_here, parts, fields, leaf = coefficients.shape
    flat = coefficients.reshape(orders_here, parts * fields, leaf)
    rows, lat = butterfly(
        flat, leaf_factors, level_interpolants, latitude_factors, parts,
        lax.axis_size("ord"), lax.axis_size("blk"),
    )
    return products_of(synthesis_table(order_ids, NLON, PERIOD), rows, lat)


def solution(mesh):
    in_specs = (
        P("ord", None, None, "blk"),
        P("ord", None, "blk"),
        P(None, None, "ord", None, "blk"),
        P("ord", "blk", None),
        P(),
    )
    out_specs = P(None, "ord", "blk")
    return jax.shard_map(
        per_device, mesh=mesh, in_specs=in_specs, out_specs=out_specs, check_vma=False
    )
```

time: 214 us -> 112 us (0.52)
  Pallas kernels: 0 us -> 109 us
  waiting for transfers between devices: 105 us -> 0 us
  matrix products: 35.5 us -> 0 us
  local copies, waits for them, and re-layouts: 31.4 us -> 0.78 us
  other arithmetic: 18.6 us -> 1.53 us
  between operations: 13.5 us -> 0.04 us
  starting transfers between devices: 9.81 us -> 0 us
    pallas_call x0 -> x2, Pallas kernels: none -> 109 us  [the longest x1 66.6 us: butterfly(): pl.pallas_call(functools.partial(butterfly_kernel, n_ord, n_blk), out_sha...]
    ppermute x3 -> x0, waiting for transfers between devices: 90.1 us -> none  [partner(): lax.ppermute(shard, axis, [(i, i ^ 1 << apart) for i in range(lax.axis_si...]
    dot_general x9 -> x0, matrix products: 35.5 us -> none  [the longest x1 24.9 us: per_device(): lax.dot_general(table, stacked_blocks, (((0,), (0,)), ((), ())), preferre...]
    convert_element_type x1 -> x0, other arithmetic: 18.4 us -> none  [per_device(): return (grid[:, :, 0, :] * grid[:, :, 1, :]).astype(jnp.bfloat16)]
    all_to_all x1 -> x0, waiting for transfers between devices: 14.1 us -> none  [per_device(): lax.all_to_all(spaced, 'ord', split_axis=2, concat_axis=0, tiled=True)]
    convert_element_type x2, local copies, waits for them, and re-layouts: 14.3 us -> 0.75 us  [synthesis_table(): return table.astype(jnp.bfloat16).reshape(count, -1)]
    dot_general x1 -> x0, local copies, waits for them, and re-layouts: 8.72 us -> none  [per_device(): lax.dot_general(table, stacked_blocks, (((0,), (0,)), ((), ())), preferre...]
    ppermute x3 -> x0, starting transfers between devices: 6.29 us -> none  [partner(): lax.ppermute(shard, axis, [(i, i ^ 1 << apart) for i in range(lax.axis_si...]
  transfers between devices with their start and end apart: 5 -> 0, of which waited for: 4 -> 0; matrix products, arithmetic and copies ran while one was open for 4% -> 0% of each run, Pallas kernels for 0% -> 0%
where the time goes in v1:
time: 112 us; the launch traced here: 111 us
  Pallas kernels  109 us (97%)
  other arithmetic  1.53 us (1%)
    pallas_call x1, Pallas kernels, butterfly(): pl.pallas_call(functools.partial(butterfly_kernel, n_ord, n_blk), out_sha...  66.6 us
    pallas_call x1, Pallas kernels, products_of(): pl.pallas_call(products_kernel, out_shape=jax.ShapeDtypeStruct((nlon, pai...  42.4 us

profile of v1, /device:TPU:0, one launch (start us, length us, event | category | flops | bytes accessed | tf_op | source)
XLA Modules:
  0.0 111.4 jit_solution(1452563790123722175)
XLA Ops:
  0.0 0.7 compare_select_fusion
  0.7 0.9 multiply_convert_fusion.1
  1.6 0.7 copy.8.table_ref
  2.3 66.6 %butterfly.1 = (bf16[32,2,64,128]{3,2,1,0:T(8,128)(2,1)}, bf16[32,640,128]{2,1,0:T(8,128)(2,1)}) custom-call(bf16[8,512,512]{2,1,0:T(8,128)(2,1)} %bitcast.3, bf16[8,128,512]{2,1,0:T(8,128)(2,1)} %leaf_hbm.1, bf16[3,2,8,128,128]{4,3,2,1,0:T(8,128)(2,1)} %interp_hbm.1, bf16[8,640,128]{2,1,0:T(8,128)(2,1)} %lat_hbm.1), custom_call_target="tpu_custom_call" | custom-call | tf_op jit(solution)/shard_map/butterfly/pallas_call | solution.py:198
  68.9 42.4 %products.1 = bf16[256,32,640]{2,1,0:T(8,128)(2,1)} custom-call(bf16[256,64]{1,0:T(8,128)(2,1)} %copy.8.table_ref, bf16[32,2,64,128]{3,2,1,0:T(8,128)(2,1)} %get-tuple-element.7.rows_ref, bf16[32,640,128]{2,1,0:T(8,128)(2,1)} %get-tuple-element.8.lat_ref), custom_call_target="tpu_custom_call" | custom-call | tf_op jit(solution)/shard_map/products/pallas_call | solution.py:263
  (3 shorter events, 0.1 us)

commit v2 on v1

--- a/solution.py
+++ b/solution.py
@@ -232,27 +232,23 @@
 
     @pl.loop(0, total, unroll=4)
     def _(m):
-        at = pl.multiple_of(m * parts * group, parts * group)
-        values[pl.ds(at, parts * group), :] = lax.dot_general(
+        values[pl.ds(m * parts, parts)] = lax.dot_general(
             rows_ref[m].reshape(parts * group, rank), lat_ref[m], NT,
             preferred_element_type=jnp.float32,
-        )
-
-    @pl.loop(0, pairs, unroll=2)
-    def _(p):
-        both = jnp.concatenate(
-            [values[pl.ds(2 * p + h, depth, stride=group), :].astype(jnp.bfloat16) for h in range(2)],
-            axis=1,
-        )
-        grid = jnp.dot(table_ref[...], both, preferred_element_type=jnp.float32)
-        mixed[pl.ds(p, nlon, stride=pairs), :] = grid[:, :lanes] * grid[:, lanes:]
-
-    @pl.loop(0, nlon // 16, unroll=2)
+        ).reshape(parts, group, lanes).astype(jnp.bfloat16)
+
+    @pl.loop(0, group // 16)
+    def _(q):
+        fields = jnp.transpose(values[:, pl.ds(pl.multiple_of(q * 16, 16), 16), :], (1, 0, 2))
+        for h in range(8):
+            both = jnp.concatenate([fields[2 * h], fields[2 * h + 1]], axis=1)
+            grid = jnp.dot(table_ref[...], both, preferred_element_type=jnp.float32)
+            mixed[q * 8 + h] = (grid[:, :lanes] * grid[:, lanes:]).astype(jnp.bfloat16)
+
+    @pl.loop(0, nlon // 16)
     def _(b):
-        at = pl.multiple_of(b * 16 * pairs, 16 * pairs)
-        out_ref[pl.ds(b * 16, 16)] = (
-            mixed[pl.ds(at, 16 * pairs), :].astype(jnp.bfloat16).reshape(16, pairs, lanes)
-        )
+        at = pl.ds(pl.multiple_of(b * 16, 16), 16)
+        out_ref[at] = jnp.transpose(mixed[:, at, :], (1, 0, 2))
 
 
 def products_of(table, rows, lat):
@@ -271,8 +267,8 @@
         ],
         out_specs=pl.BlockSpec((nlon, pairs, LANES), lambda t: (0, 0, t)),
         scratch_shapes=[
-            pltpu.VMEM((total * parts * group, LANES), jnp.float32),
-            pltpu.VMEM((nlon * pairs, LANES), jnp.float32),
+            pltpu.VMEM((total * parts, group, LANES), jnp.bfloat16),
+            pltpu.VMEM((pairs, nlon, LANES), jnp.bfloat16),
         ],
         name="products",
     )(table, rows, lat)

time: 112 us -> 94 us (0.84)
  Pallas kernels: 109 us -> 91.5 us
    pallas_call x1, Pallas kernels: 42.4 us -> 24.9 us  [products_of(): pl.pallas_call(products_kernel, out_shape=jax.ShapeDtypeStruct((nlon, pai...]
where the time goes in v2:
time: 94 us; the launch traced here: 93.9 us
  Pallas kernels  91.5 us (97%)
  other arithmetic  1.53 us (2%)
    pallas_call x1, Pallas kernels, butterfly(): pl.pallas_call(functools.partial(butterfly_kernel, n_ord, n_blk), out_sha...  66.6 us
    pallas_call x1, Pallas kernels, products_of(): pl.pallas_call(products_kernel, out_shape=jax.ShapeDtypeStruct((nlon, pai...  24.9 us

profile of v2, /device:TPU:0, one launch (start us, length us, event | category | flops | bytes accessed | tf_op | source)
XLA Modules:
  0.0 93.9 jit_solution(12916103777908739906)
XLA Ops:
  0.0 0.7 compare_select_fusion
  0.7 0.9 multiply_convert_fusion.1
  1.6 0.7 copy.8.table_ref
  2.3 66.6 %butterfly.1 = (bf16[32,2,64,128]{3,2,1,0:T(8,128)(2,1)}, bf16[32,640,128]{2,1,0:T(8,128)(2,1)}) custom-call(bf16[8,512,512]{2,1,0:T(8,128)(2,1)} %bitcast.3, bf16[8,128,512]{2,1,0:T(8,128)(2,1)} %leaf_hbm.1, bf16[3,2,8,128,128]{4,3,2,1,0:T(8,128)(2,1)} %interp_hbm.1, bf16[8,640,128]{2,1,0:T(8,128)(2,1)} %lat_hbm.1), custom_call_target="tpu_custom_call" | custom-call | tf_op jit(solution)/shard_map/butterfly/pallas_call | solution.py:198
  68.9 24.9 %products.1 = bf16[256,32,640]{2,1,0:T(8,128)(2,1)} custom-call(bf16[256,64]{1,0:T(8,128)(2,1)} %copy.8.table_ref, bf16[32,2,64,128]{3,2,1,0:T(8,128)(2,1)} %get-tuple-element.7.rows_ref, bf16[32,640,128]{2,1,0:T(8,128)(2,1)} %get-tuple-element.8.lat_ref), custom_call_target="tpu_custom_call" | custom-call | tf_op jit(solution)/shard_map/products/pallas_call | solution.py:259
  (3 shorter events, 0.1 us)

commit v3 on v2

v3 whole, which is shorter than its diff:
```python
import functools
import math

import jax
import jax.numpy as jnp
from jax import lax
from jax.experimental import pallas as pl
from jax.experimental.pallas import tpu as pltpu
from jax.sharding import PartitionSpec as P

PERIOD = 16384
NLON = 256
LANES = 128
WINDOW = 4
LEVEL_LAG = 3
MESH = pl.DeviceIdType.MESH
NT = (((1,), (1,)), ((), ()))


def synthesis_table(order_ids, count, period):
    steps = lax.broadcasted_iota(jnp.int32, (count, order_ids.shape[1]), 0)
    phase = lax.rem(steps * order_ids, period).astype(jnp.float32) * (2.0 * math.pi / period)
    weight = jnp.where(order_ids == 0, 1.0, 2.0).astype(jnp.float32)
    table = jnp.concatenate([weight * jnp.cos(phase), -weight * jnp.sin(phase)], axis=1)
    return table.astype(jnp.bfloat16)


def butterfly_kernel(
    n_ord, n_blk, coef_hbm, leaf_hbm, interp_hbm, lat_hbm, ids_ref,
    rows_out, lat_out, table_ref,
    coef, leaf, interp, lat, own, came,
    in_sem, level_send, level_recv, group_send, group_recv, own_sem,
    lat_send, lat_recv, lat_pass,
):
    me_ord, me_blk = lax.axis_index("ord"), lax.axis_index("blk")
    orders, parts, _, _ = coef.shape
    levels = interp.shape[0]
    chunks = orders * parts
    group = rows_out.shape[2]

    lat_in = pltpu.make_async_copy(lat_hbm, lat, in_sem.at[2, 0])
    interp_in = pltpu.make_async_copy(interp_hbm, interp, in_sem.at[2, 1])

    def order_in(i):
        return (
            pltpu.make_async_copy(coef_hbm.at[i], coef.at[i], in_sem.at[0, i]),
            pltpu.make_async_copy(leaf_hbm.at[i], leaf.at[i], in_sem.at[1, i]),
        )

    for i in range(orders):
        for copy in order_in(i):
            copy.start()
        if i == 1:
            interp_in.start()
            lat_in.start()

    barrier = pltpu.get_barrier_semaphore()
    partners = [me_blk ^ (n_blk >> (k + 1)) for k in range(levels)]
    for k in range(levels):
        pl.semaphore_signal(barrier, inc=1, device_id={"blk": partners[k]}, device_id_type=MESH)
    for d in range(1, n_ord):
        pl.semaphore_signal(
            barrier, inc=1, device_id={"ord": lax.rem(me_ord + d, n_ord)}, device_id_type=MESH
        )

    def leaf_step(c):
        i, part = c // parts, lax.rem(c, parts)

        @pl.when(part == 0)
        def _():
            for copy in order_in(i):
                copy.wait()

        own[0, c] = lax.dot_general(
            coef[i, part], leaf[i], NT, preferred_element_type=jnp.float32
        ).astype(jnp.bfloat16)

    leaf_step(0)
    pl.semaphore_wait(barrier, levels + n_ord - 1)

    def level_copy(k, c):
        return pltpu.make_async_remote_copy(
            src_ref=own.at[k, c], dst_ref=came.at[k, c],
            send_sem=level_send.at[k, c], recv_sem=level_recv.at[k, c],
            device_id={"blk": partners[k]}, device_id_type=MESH,
        )

    def group_rows(c, g):
        return own.at[levels, c, pl.ds(pl.multiple_of(g * group, group), group)]

    def landing(c):
        return rows_out.at[me_ord * orders + c // parts, lax.rem(c, parts)]

    def group_copy(c, d):
        peer = lax.rem(me_ord + d, n_ord)
        return pltpu.make_async_remote_copy(
            src_ref=group_rows(c, peer), dst_ref=landing(c),
            send_sem=group_send.at[c, d], recv_sem=group_recv.at[c, d],
            device_id={"ord": peer}, device_id_type=MESH,
        )

    def own_copy(c):
        return pltpu.make_async_copy(group_rows(c, me_ord), landing(c), own_sem.at[c])

    def lat_rows(o):
        return lat_out.at[pl.ds(o * orders, orders)]

    half = n_ord // 2
    mate = me_ord ^ 1

    def lat_copy(d):
        target = mate if d == 0 else lax.rem(me_ord + 2 * d, n_ord)
        return pltpu.make_async_remote_copy(
            src_ref=lat, dst_ref=lat_rows(me_ord),
            send_sem=lat_send.at[d], recv_sem=lat_recv.at[d],
            device_id={"ord": target}, device_id_type=MESH,
        )

    def lat_forward(d):
        source = lax.rem(me_ord + n_ord - 2 * d, n_ord)
        return pltpu.make_async_remote_copy(
            src_ref=lat_rows(source), dst_ref=lat_rows(source),
            send_sem=lat_pass.at[d], recv_sem=lat_recv.at[half + d],
            device_id={"ord": mate}, device_id_type=MESH,
        )

    lat_own = pltpu.make_async_copy(lat, lat_rows(me_ord), in_sem.at[2, 2])

    level_copy(0, 0).start()

    @pl.loop(1, WINDOW)
    def _(c):
        leaf_step(c)
        level_copy(0, c).start()

    lat_in.wait()
    for d in range(half):
        lat_copy(d).start()
    lat_own.start()
    interp_in.wait()
    table_ref[...] = synthesis_table(ids_ref[...], table_ref.shape[0], PERIOD)

    def level_step(k, c):
        i = c // parts
        level_copy(k, c).wait_recv()
        mixed = lax.dot_general(
            own[k, c], interp[k, 0, i], NT, preferred_element_type=jnp.float32
        ) + lax.dot_general(
            came[k, c], interp[k, 1, i], NT, preferred_element_type=jnp.float32
        )
        own[k + 1, c] = mixed.astype(jnp.bfloat16)
        if k + 1 < levels:
            level_copy(k + 1, c).start()
        else:
            for d in range(1, n_ord):
                group_copy(c, d).start()
            own_copy(c).start()

    @pl.loop(0, chunks + LEVEL_LAG * (levels - 1))
    def _(s):
        @pl.when(s + WINDOW < chunks)
        def _():
            leaf_step(s + WINDOW)

        for k in range(levels):
            c = s - k * LEVEL_LAG

            @pl.when((c >= 0) & (c < chunks))
            def _():
                level_step(k, c)

            if k == 0:
                @pl.when(s + WINDOW < chunks)
                def _():
                    level_copy(0, s + WINDOW).start()

        @pl.when(s == chunks - 3)
        def _():
            for d in range(1, half):
                lat_copy(d).wait_recv()
                lat_forward(d).start()

    lat_copy(0).wait_recv()
    for d in range(1, half):
        lat_forward(d).wait_recv()
    for d in range(half):
        lat_copy(d).wait_send()
    for d in range(1, half):
        lat_forward(d).wait_send()
    lat_own.wait()

    @pl.loop(0, chunks)
    def _(c):
        for k in range(levels):
            level_copy(k, c).wait_send()
        for d in range(1, n_ord):
            group_copy(c, d).wait_recv()
            group_copy(c, d).wait_send()
        own_copy(c).wait()


def butterfly(coefficients, leaf_factors, interpolants, latitude_factors, order_ids, n_ord, n_blk):
    orders, parts, fields, _ = coefficients.shape
    rank = leaf_factors.shape[1]
    levels = interpolants.shape[0]
    lats = latitude_factors.shape[1]
    chunks = orders * parts
    total = n_ord * orders
    any_spec = pl.BlockSpec(memory_space=pl.ANY)
    vmem_spec = pl.BlockSpec(memory_space=pltpu.VMEM)
    dma = pltpu.SemaphoreType.DMA
    return pl.pallas_call(
        functools.partial(butterfly_kernel, n_ord, n_blk),
        out_shape=(
            jax.ShapeDtypeStruct((total, parts, fields // n_ord, rank), jnp.bfloat16),
            jax.ShapeDtypeStruct((total, lats, rank), jnp.bfloat16),
            jax.ShapeDtypeStruct((NLON, parts * total), jnp.bfloat16),
        ),
        in_specs=[any_spec] * 4 + [vmem_spec],
        out_specs=(any_spec, any_spec, vmem_spec),
        scratch_shapes=[
            pltpu.VMEM(coefficients.shape, jnp.bfloat16),
            pltpu.VMEM(leaf_factors.shape, jnp.bfloat16),
            pltpu.VMEM(interpolants.shape, jnp.bfloat16),
            pltpu.VMEM(latitude_factors.shape, jnp.bfloat16),
            pltpu.VMEM((levels + 1, chunks, fields, rank), jnp.bfloat16),
            pltpu.VMEM((levels, chunks, fields, rank), jnp.bfloat16),
            dma((3, max(orders, 3))),
            dma((levels, chunks)),
            dma((levels, chunks)),
            dma((chunks, n_ord)),
            dma((chunks, n_ord)),
            dma((chunks,)),
            dma((n_ord,)),
            dma((n_ord,)),
            dma((n_ord,)),
        ],
        compiler_params=pltpu.CompilerParams(collective_id=0, has_side_effects=True),
        name="butterfly",
    )(coefficients, leaf_factors, interpolants, latitude_factors, order_ids[None, :])


def products_kernel(table_ref, rows_ref, lat_ref, out_ref, values, mixed):
    total, parts, group, rank = rows_ref.shape
    nlon, pairs, lanes = out_ref.shape
    depth = total * parts

    @pl.loop(0, total, unroll=8)
    def _(m):
        mapped = lax.dot_general(
            rows_ref[m].reshape(parts * group, rank), lat_ref[m], NT,
            preferred_element_type=jnp.float32,
        ).reshape(parts, group, lanes).astype(jnp.bfloat16)
        for part in range(parts):
            values[part * total + m] = mapped[part]

    @pl.loop(0, group // 16, unroll=True)
    def _(q):
        fields = jnp.transpose(values[:, pl.ds(pl.multiple_of(q * 16, 16), 16), :], (1, 0, 2))
        for h in range(8):
            both = jnp.concatenate([fields[2 * h], fields[2 * h + 1]], axis=1)
            grid = jnp.dot(table_ref[...], both, preferred_element_type=jnp.float32)
            mixed[q * 8 + h] = (grid[:, :lanes] * grid[:, lanes:]).astype(jnp.bfloat16)

    @pl.loop(0, nlon // 16, unroll=4)
    def _(b):
        at = pl.ds(pl.multiple_of(b * 16, 16), 16)
        out_ref[at] = jnp.transpose(mixed[:, at, :], (1, 0, 2))


def products_of(table, rows, lat):
    total, parts, group, rank = rows.shape
    lats = lat.shape[1]
    pairs = group // 2
    nlon = table.shape[0]
    return pl.pallas_call(
        products_kernel,
        out_shape=jax.ShapeDtypeStruct((nlon, pairs, lats), jnp.bfloat16),
        grid=(lats // LANES,),
        in_specs=[
            pl.BlockSpec(table.shape, lambda t: (0, 0)),
            pl.BlockSpec(rows.shape, lambda t: (0, 0, 0, 0)),
            pl.BlockSpec((total, LANES, rank), lambda t: (0, t, 0)),
        ],
        out_specs=pl.BlockSpec((nlon, pairs, LANES), lambda t: (0, 0, t)),
        scratch_shapes=[
            pltpu.VMEM((total * parts, group, LANES), jnp.bfloat16),
            pltpu.VMEM((pairs, nlon, LANES), jnp.bfloat16),
        ],
        name="products",
    )(table, rows, lat)


def per_device(coefficients, leaf_factors, level_interpolants, latitude_factors, order_ids):
    rows, lat, table = butterfly(
        coefficients, leaf_factors, level_interpolants, latitude_factors, order_ids,
        lax.axis_size("ord"), lax.axis_size("blk"),
    )
    return products_of(table, rows, lat)


def solution(mesh):
    in_specs = (
        P("ord", None, None, "blk"),
        P("ord", None, "blk"),
        P(None, None, "ord", None, "blk"),
        P("ord", "blk", None),
        P(),
    )
    out_specs = P(None, "ord", "blk")
    return jax.shard_map(
        per_device, mesh=mesh, in_specs=in_specs, out_specs=out_specs, check_vma=False
    )
```

time: 94 us -> 84.8 us (0.902)
  Pallas kernels: 91.5 us -> 84.7 us
  other arithmetic: 1.53 us -> 0 us
    pallas_call x1, Pallas kernels: 24.9 us -> 18.8 us  [products_of(): pl.pallas_call(products_kernel, out_shape=jax.ShapeDtypeStruct((nlon, pai...]
where the time goes in v3:
time: 84.8 us; the launch traced here: 84.7 us
  Pallas kernels  84.7 us (100%)
    pallas_call x1, Pallas kernels, butterfly(): pl.pallas_call(functools.partial(butterfly_kernel, n_ord, n_blk), out_sha...  65.8 us
    pallas_call x1, Pallas kernels, products_of(): pl.pallas_call(products_kernel, out_shape=jax.ShapeDtypeStruct((nlon, pai...  18.8 us

profile of v3, /device:TPU:0, one launch (start us, length us, event | category | flops | bytes accessed | tf_op | source)
XLA Modules:
  0.0 84.7 jit_solution(15743433781216900415)
XLA Ops:
  0.0 65.8 %butterfly.1 = (bf16[32,2,64,128]{3,2,1,0:T(8,128)(2,1)}, bf16[32,640,128]{2,1,0:T(8,128)(2,1)}, bf16[256,64]{1,0:T(8,128)(2,1)}) custom-call(bf16[8,2,256,512]{3,2,1,0:T(8,128)(2,1)} %coef_hbm.1, bf16[8,128,512]{2,1,0:T(8,128)(2,1)} %leaf_hbm.1, bf16[3,2,8,128,128]{4,3,2,1,0:T(8,128)(2,1)} %interp_hbm.1, bf16[8,640,128]{2,1,0:T(8,128)(2,1)} %lat_hbm.1, ...), custom_call_target="tpu_custom_call" | custom-call | tf_op jit(solution)/shard_map/butterfly/pallas_call | solution.py:212
  65.9 18.8 %products.1 = bf16[256,32,640]{2,1,0:T(8,128)(2,1)} custom-call(bf16[256,64]{1,0:T(8,128)(2,1)} %get-tuple-element.8.table_ref, bf16[32,2,64,128]{3,2,1,0:T(8,128)(2,1)} %get-tuple-element.9.rows_ref, bf16[32,640,128]{2,1,0:T(8,128)(2,1)} %get-tuple-element.10.lat_ref), custom_call_target="tpu_custom_call" | custom-call | tf_op jit(solution)/shard_map/products/pallas_call | solution.py:276

commit v4 on v3

--- a/solution.py
+++ b/solution.py
@@ -245,7 +245,7 @@
     nlon, pairs, lanes = out_ref.shape
     depth = total * parts
 
-    @pl.loop(0, total, unroll=8)
+    @pl.loop(0, total, unroll=32)
     def _(m):
         mapped = lax.dot_general(
             rows_ref[m].reshape(parts * group, rank), lat_ref[m], NT,

time: 84.8 us -> 82.9 us (0.978)
  Pallas kernels: 84.7 us -> 82.7 us
    pallas_call x1, Pallas kernels: 18.8 us -> 16.9 us  [products_of(): pl.pallas_call(products_kernel, out_shape=jax.ShapeDtypeStruct((nlon, pai...]
where the time goes in v4:
time: 82.9 us; the launch traced here: 82.7 us
  Pallas kernels  82.7 us (100%)
    pallas_call x1, Pallas kernels, butterfly(): pl.pallas_call(functools.partial(butterfly_kernel, n_ord, n_blk), out_sha...  65.8 us
    pallas_call x1, Pallas kernels, products_of(): pl.pallas_call(products_kernel, out_shape=jax.ShapeDtypeStruct((nlon, pai...  16.9 us

profile of v4, /device:TPU:0, one launch (start us, length us, event | category | flops | bytes accessed | tf_op | source)
XLA Modules:
  0.0 82.7 jit_solution(9318441890459403578)
XLA Ops:
  0.0 65.8 %butterfly.1 = (bf16[32,2,64,128]{3,2,1,0:T(8,128)(2,1)}, bf16[32,640,128]{2,1,0:T(8,128)(2,1)}, bf16[256,64]{1,0:T(8,128)(2,1)}) custom-call(bf16[8,2,256,512]{3,2,1,0:T(8,128)(2,1)} %coef_hbm.1, bf16[8,128,512]{2,1,0:T(8,128)(2,1)} %leaf_hbm.1, bf16[3,2,8,128,128]{4,3,2,1,0:T(8,128)(2,1)} %interp_hbm.1, bf16[8,640,128]{2,1,0:T(8,128)(2,1)} %lat_hbm.1, ...), custom_call_target="tpu_custom_call" | custom-call | tf_op jit(solution)/shard_map/butterfly/pallas_call | solution.py:212
  65.9 16.9 %products.1 = bf16[256,32,640]{2,1,0:T(8,128)(2,1)} custom-call(bf16[256,64]{1,0:T(8,128)(2,1)} %get-tuple-element.8.table_ref, bf16[32,2,64,128]{3,2,1,0:T(8,128)(2,1)} %get-tuple-element.9.rows_ref, bf16[32,640,128]{2,1,0:T(8,128)(2,1)} %get-tuple-element.10.lat_ref), custom_call_target="tpu_custom_call" | custom-call | tf_op jit(solution)/shard_map/products/pallas_call | solution.py:276
